TPU v7x, 32 devices: a whole 2x2x4 slice. The times are simulated.
32 devices in a mesh: cfg: 2 (over y), space: 4 (over z), tm: 4 (over x, core).
Axes of the slice: x: 2, y: 2, z: 4, core: 2. Of those that a mesh axis runs over, the one named last changes fastest.
Arguments:
- eigenvectors: bfloat16 [8, 2, 3, 3072, 384], P(('cfg', 'tm'), None, None, 'space'), parts along dimension 0, may hold values from -6 to 6
- perambulator: bfloat16 [8, 2, 1536, 1536], P(('cfg', 'tm'), None, None, 'space'), parts along dimension 0, may hold values from -0.3125 to 0.3125
- momenta: int32 [2, 3], replicated, may hold values from -2 to 2
- ratios: int32 [2, 2], replicated, may hold values from 1 to 3
- source_slice: int32 [1], replicated, may hold values from 0 to 255
Outputs:
- meson_blocks: float32 [8, 2, 1536, 1536], P(('cfg', 'tm'), None, 'space'), parts along dimension 0
There are 2 independent parts, one for each index of `cfg`. A program takes and returns all parts, laid end to end along the dimension named above; an argument that names none is the same for every part. Nothing has to cross between parts.
Inputs may be any that keep to these rules, and one draw needn't show every extreme that they name: `momenta`: row k is momentum k in units of 2 pi / 64. `ratios`: row k holds the numerator (column 0) and the denominator (column 1) of momentum k's coefficient.
All inputs are finite; a program needn't handle non-finite values.
Results may differ from a plain program's by a relative error of at most 0.0063.
Values may be sent and summed in bfloat16 or wider, within the bound.
No kernel may reach another device: no remote copies, remote signals or barrier semaphores. Data moves between devices by JAX's collectives and lax.ppermute only.
A program may use at most 64 MiB of HBM per device.

v0:
```python
import math

import jax
import jax.numpy as jnp
from jax import lax
from jax.sharding import PartitionSpec as P

LSIDE = 64


def spread(value, axis, source):
    kept = jnp.where(lax.axis_index(axis) == source, value, 0).astype(value.dtype)
    return lax.psum(kept, axis)


def site_phases(momenta, first_site, site_count):
    site_index = first_site + lax.iota(jnp.int32, site_count)
    along_x = site_index % LSIDE
    along_y = site_index // LSIDE % LSIDE
    along_z = site_index // (LSIDE * LSIDE)
    turn_count = (
        momenta[:, 0:1] * along_x[None, :]
        + momenta[:, 1:2] * along_y[None, :]
        + momenta[:, 2:3] * along_z[None, :]
    )
    phase_angle = (turn_count % LSIDE).astype(jnp.float32) * (2.0 * math.pi / LSIDE)
    return (jnp.cos(phase_angle), jnp.sin(phase_angle))


def split_elementals(product, vector_count):
    lead_shape = product.shape[:-2]
    product_grid = product.reshape(lead_shape + (2, vector_count, 2, 2, vector_count))
    real_part = product_grid[..., 0, :, :, 0, :] + product_grid[..., 1, :, :, 1, :]
    imaginary = product_grid[..., 0, :, :, 1, :] - product_grid[..., 1, :, :, 0, :]
    stacked = jnp.stack([real_part, imaginary], axis=-4)
    return jnp.moveaxis(stacked, -2, -4)


def elementals(vectors, cosine, sine_part):
    slab_count, color_count, site_count, vector_count = (
        vectors.shape[0],
        vectors.shape[2],
        vectors.shape[3],
        vectors.shape[4],
    )
    row_count = color_count * site_count
    real_rows = vectors[:, 0].reshape(slab_count, row_count, vector_count)
    imaginary_rows = vectors[:, 1].reshape(slab_count, row_count, vector_count)
    cos_rows = jnp.broadcast_to(cosine[:, None, :], (2, color_count, site_count)).reshape(
        1, 2, row_count, 1
    )
    sin_rows = jnp.broadcast_to(sine_part[:, None, :], (2, color_count, site_count)).reshape(
        1, 2, row_count, 1
    )
    phased_real = (cos_rows * real_rows[:, None] + sin_rows * imaginary_rows[:, None]).astype(
        jnp.bfloat16
    )
    phased_imaginary = (cos_rows * imaginary_rows[:, None] - sin_rows * real_rows[:, None]).astype(
        jnp.bfloat16
    )
    phased = jnp.concatenate([phased_real, phased_imaginary], axis=3)
    phased = jnp.transpose(phased, (0, 2, 1, 3)).reshape(slab_count, row_count, 4 * vector_count)
    plain_vectors = jnp.concatenate([real_rows, imaginary_rows], axis=2)
    product = lax.dot_general(
        plain_vectors, phased, (((1,), (1,)), ((0,), (0,))), preferred_element_type=jnp.float32
    )
    return split_elementals(product, vector_count)


def source_block(chosen):
    real_t = chosen[0].T
    imaginary_t = chosen[1].T
    upper = jnp.concatenate([real_t, -imaginary_t], axis=1)
    lower = jnp.concatenate([imaginary_t, real_t], axis=1)
    return jnp.concatenate([upper, lower], axis=0)


def propagate(sink_matrix, tau):
    vector_count = sink_matrix.shape[1]
    spin_count = tau.shape[1] // vector_count
    column_count = tau.shape[2]
    real_part, imaginary = (sink_matrix[0], sink_matrix[1])
    upper = jnp.concatenate([real_part, -imaginary], axis=1)
    lower = jnp.concatenate([imaginary, real_part], axis=1)
    sink_big = jnp.concatenate([upper, lower], axis=0)
    stacked = jnp.transpose(tau.reshape(2, spin_count, vector_count, column_count), (0, 2, 1, 3))
    stacked = stacked.reshape(2 * vector_count, spin_count * column_count)
    product = jnp.dot(sink_big, stacked, preferred_element_type=jnp.float32)
    product = jnp.transpose(
        product.reshape(2, vector_count, spin_count, column_count), (0, 2, 1, 3)
    )
    return product.reshape(2, spin_count * vector_count, column_count).astype(jnp.bfloat16)


def attach_source(propagated, source_big):
    vector_count = source_big.shape[0] // 2
    row_count = propagated.shape[1]
    spin_count = propagated.shape[2] // vector_count
    stacked = jnp.concatenate(
        [
            propagated[0].reshape(row_count, spin_count, vector_count),
            propagated[1].reshape(row_count, spin_count, vector_count),
        ],
        axis=2,
    )
    product = jnp.dot(
        stacked.reshape(row_count * spin_count, 2 * vector_count),
        source_big,
        preferred_element_type=jnp.float32,
    )
    product = jnp.transpose(product.reshape(row_count, spin_count, 2, vector_count), (2, 0, 1, 3))
    return product.reshape(2, row_count, spin_count * vector_count)


def body(eigenvectors, perambulator, momenta, ratios, source_slice):
    slab_count = eigenvectors.shape[0]
    color_count = eigenvectors.shape[2]
    site_count = eigenvectors.shape[3]
    vector_count = eigenvectors.shape[4]
    first_site = lax.axis_index("space") * site_count
    cosine, sine_part = site_phases(momenta, first_site, site_count)
    normalizer = 1.0 / math.sqrt(color_count * site_count * lax.axis_size("space") * vector_count)
    weights = (
        ratios[:, 0].astype(jnp.float32) / ratios[:, 1].astype(jnp.float32) * normalizer
    ).reshape(1, 2, 1, 1, 1)
    parts = elementals(eigenvectors, cosine, sine_part)
    partial_sums = jnp.sum(weights * parts, axis=1, keepdims=True)
    summed = lax.psum(partial_sums, "space")
    sink_matrices = summed[:, 0].astype(jnp.bfloat16)
    global_slice = source_slice[0] % (slab_count * lax.axis_size("tm"))
    local_source = lax.dynamic_index_in_dim(
        sink_matrices, global_slice % slab_count, 0, keepdims=False
    )
    chosen = spread(local_source, "tm", global_slice // slab_count)
    source_big = source_block(chosen)
    propagated = jnp.stack([propagate(sink_matrices[0], perambulator[0])])
    return jnp.stack(
        [
            attach_source(
                lax.all_to_all(propagated, "space", split_axis=2, concat_axis=3, tiled=True)[0],
                source_big,
            )
        ]
    )


def solution(mesh):
    placed = (
        P(("cfg", "tm"), None, None, "space", None),
        P(("cfg", "tm"), None, None, "space"),
        P(),
        P(),
        P(),
    )
    return jax.shard_map(
        body,
        mesh=mesh,
        in_specs=placed,
        out_specs=P(("cfg", "tm"), None, "space", None),
        check_vma=False,
    )
```

profile of v0, /device:TPU:0, one launch (start us, length us, event | category | flops | bytes accessed | tf_op | source)
XLA Modules:
  0.0 198.8 jit_solution(15958804307998417582)
XLA Ops:
  6.6 1.0 slice_reduce_fusion.2
  7.9 0.6 copy.41
  8.5 0.6 copy.40
  9.1 2.4 %fusion.23 = (bf16[1,1,3,768,384]{4,3,2,1,0:T(8,128)(2,1)S(1)}, bf16[1,1,3,768,384]{4,3,2,1,0:T(8,128)(2,1)S(1)}) fusion(bf16[1,2,3,768,384]{4,3,2,1,0:T(8,128)(2,1)} %param.5), kind=kLoop, calls=%fused_computation.68 | loop fusion | bytes 7077888 | tf_op jit(solution)/shard_map/slice | solution.py:47
  11.5 3.8 %bitcast_convert_fusion = (f32[2304,384]{1,0:T(8,128)}, f32[2304,384]{1,0:T(8,128)}) fusion(bf16[1,1,3,768,384]{4,3,2,1,0:T(8,128)(2,1)S(1)} %get-tuple-element.13, bf16[1,1,3,768,384]{4,3,2,1,0:T(8,128)(2,1)S(1)} %get-tuple-element.12), kind=kLoop, calls=%fused_computation.13 | loop fusion | flops 1769472 | bytes 10616832 | tf_op jit(solution)/shard_map/convert_element_type | solution.py:55
  15.3 5.2 %copy.24 = f32[2304,384]{0,1:T(8,128)} copy(f32[2304,384]{1,0:T(8,128)} %get-tuple-element.21) | data formatting | bytes 7077888 | tf_op jit(solution)/shard_map/convert_element_type | solution.py:55
  20.4 5.2 %copy.25 = f32[2304,384]{0,1:T(8,128)} copy(f32[2304,384]{1,0:T(8,128)} %get-tuple-element.20) | data formatting | bytes 7077888 | tf_op jit(solution)/shard_map/convert_element_type | solution.py:55
  25.6 2.4 %copy.22 = bf16[1,2304,384]{1,2,0:T(8,128)(2,1)} copy(bf16[1,2304,384]{2,1,0:T(8,128)(2,1)S(1)} %bitcast.121) | data formatting | bytes 3538944 | tf_op jit(solution)/shard_map/reshape;squeeze | solution.py:47
  28.0 2.4 %copy.23 = bf16[1,2304,384]{1,2,0:T(8,128)(2,1)} copy(bf16[1,2304,384]{2,1,0:T(8,128)(2,1)S(1)} %bitcast.120) | data formatting | bytes 3538944 | tf_op jit(solution)/shard_map/reshape;squeeze | solution.py:48
  30.4 5.2 %add_convert_fusion = (bf16[1,2,2304,384]{2,3,1,0:T(8,128)(2,1)S(1)}, bf16[1,2,2304,384]{2,3,1,0:T(8,128)(2,1)}) fusion(f32[2304,384]{0,1:T(8,128)} %copy.25, f32[2,2304]{1,0:T(2,128)S(1)} %bitcast.135, f32[2304,384]{0,1:T(8,128)} %copy.24, f32[2,2304]{1,0:T(2,128)S(1)} %bitcast.136), kind=kLoop, calls=%fused_computation.2 | loop fusion | flops 14155776 | bytes 14192640 | tf_op jit(solution)/shard_map/convert_element_type | solution.py:55
  35.6 5.5 %pad_maximum_fusion = bf16[1,2,2304,768]{2,3,1,0:T(8,128)(2,1)} fusion(bf16[1,2,2304,384]{2,3,1,0:T(8,128)(2,1)} %get-tuple-element.11, bf16[1,2,2304,384]{2,3,1,0:T(8,128)(2,1)S(1)} %get-tuple-element.10), kind=kLoop, calls=%fused_computation | loop fusion | flops 14155776 | bytes 14155776 | tf_op jit(solution)/shard_map/concatenate | solution.py:61
  41.1 1.9 pad_maximum_fusion.1
  43.0 1.7 copy-done.1
  44.6 5.7 %convolution_bitcast_fusion = f32[1,2,384,2,2,384]{5,2,4,3,1,0:T(8,128)S(1)} fusion(bf16[2,384,2304,1,1]{2,1,4,3,0:T(8,128)(2,1)S(1)} %bitcast.129, bf16[2,2,384,2304,1]{3,2,1,0,4:T(8,128)(2,1)S(1)} %bitcast.127), kind=kOutput, calls=%fused_computation.11 | convolution fusion | flops 5435817984 | bytes 15335424 | tf_op jit(solution)/shard_map/dot_general | solution.py:64
  50.6 0.5 copy-done.4
  51.6 49.0 %all-reduce.4 = bf16[1,1,2,384,384]{4,3,2,1,0:T(8,128)(2,1)S(1)} all-reduce(f32[1,1,2,384,384]{4,3,2,1,0:T(8,128)S(1)} %bitcast.128), channel_id=1, replica_groups=mesh['cfg'=2,'space'=4,'tm'=4] {'space'}, use_global_device_ids=true, to_apply=%region_1.2 | all-reduce | flops 294912 | bytes 1769472 | tf_op jit(solution)/shard_map/psum | solution.py:128
  100.6 0.8 slice_bitcast_fusion.6
  101.4 3.5 %copy.28 = bf16[2,4,384,384]{3,1,2,0:T(4,128)(2,1)S(1)} copy(bf16[2,4,384,384]{3,2,1,0:T(8,128)(2,1)} %bitcast.130) | data formatting | bytes 4718592 | tf_op jit(solution)/shard_map/reshape;squeeze | solution.py:86
  104.9 0.4 copy.42
  105.3 2.4 %copy.37 = bf16[1536,768]{1,0:T(8,128)(2,1)} copy(bf16[1536,768]{0,1:T(8,128)(2,1)S(1)} %bitcast.123) | data formatting | bytes 4718592 | tf_op jit(solution)/shard_map/dot_general | solution.py:88
  107.7 1.1 maximum_maximum_fusion
  108.9 3.9 %convolution_convert_fusion = bf16[2,384,4,384]{3,1,2,0:T(8,128)(2,1)S(1)} fusion(bf16[2,384,768,1]{2,1,3,0:T(8,128)(2,1)S(1)} %bitcast.134, bf16[4,384,768,1]{2,1,0,3:T(8,128)(2,1)} %bitcast.131), kind=kOutput, calls=%fused_computation.12 | convolution fusion | flops 1813118976 | bytes 5898240 | tf_op jit(solution)/shard_map/dot_general | solution.py:88
  112.8 12.6 %copy.30 = bf16[1,2,1536,384]{3,1,0,2:T(2,128)(2,1)} copy(bf16[1,2,1536,384]{3,2,1,0:T(8,128)(2,1)S(1)} %bitcast.132) | data formatting | bytes 4718592 | tf_op jit(solution)/shard_map/convert_element_type | solution.py:92
  125.4 3.6 %all-to-all-start = ((bf16[1,2,1536,384]{3,1,0,2:T(2,128)(2,1)}), bf16[1,2,1536,384]{3,1,0,2:T(2,128)(2,1)S(1)}, u32[]{:S(2)}, u32[]{:S(2)}) async-start(bf16[1,2,1536,384]{3,1,0,2:T(2,128)(2,1)} %copy.30), calls=%async_computation | async-start | bytes 4718592 | tf_op jit(solution)/shard_map/all_to_all | solution.py:140
  129.8 0.9 select_bitcast_fusion
  130.7 36.8 %all-reduce.3.cloned.1.call-done = bf16[2,384,384]{2,1,0:T(8,128)(2,1)} async-done(((bf16[2,384,384]{2,1,0:T(8,128)(2,1)}), bf16[2,384,384]{2,1,0:T(8,128)(2,1)}) %all-reduce.3.cloned.1.call-update) | async-done | bytes 589840 | tf_op jit(solution)/shard_map/psum | solution.py:13
  167.5 1.0 fusion.20
  168.5 1.1 slice_bitcast_fusion.4
  169.7 11.2 %all-to-all-done = bf16[1,2,1536,384]{3,1,0,2:T(2,128)(2,1)S(1)} async-done(((bf16[1,2,1536,384]{3,1,0,2:T(2,128)(2,1)}), bf16[1,2,1536,384]{3,1,0,2:T(2,128)(2,1)S(1)}, u32[]{:S(2)}, u32[]{:S(2)}) %all-to-all-start) | async-done | bytes 2359328 | tf_op jit(solution)/shard_map/all_to_all | solution.py:140
  181.4 2.0 %fusion.4 = f32[2,384,4,384]{1,3,0,2:T(8,128)S(1)} fusion(bf16[2,384,768,1]{2,1,0,3:T(8,128)(2,1)S(1)} %bitcast.133, bf16[384,4,384]{2,0,1:T(8,128)(2,1)S(1)} %get-tuple-element.15, bf16[384,4,384]{2,0,1:T(8,128)(2,1)S(1)} %get-tuple-element.14), kind=kOutput, calls=%fused_computation.10 | convolution fusion | flops 1816657920 | bytes 8257536 | tf_op jit(solution)/shard_map/dot_general | solution.py:106
  183.5 2.4 %copy.32 = f32[2,384,4,384]{1,3,2,0:T(8,128)} copy(f32[2,384,4,384]{1,3,0,2:T(8,128)S(1)} %fusion.4) | data formatting | bytes 9437184 | tf_op jit(solution)/shard_map/transpose | solution.py:111
  185.9 6.0 %copy.33 = f32[1,2,384,1536]{3,2,1,0:T(8,128)} copy(f32[1,2,384,1536]{2,3,1,0:T(8,128)} %bitcast.119) | data formatting | bytes 9437184 | tf_op jit(solution)/shard_map/stack;reshape | solution.py:137
  (24 shorter events, 1.8 us)
Async XLA Ops:
  28.0 2.4 %copy-start.2 = (f32[1,2,3,768]{3,1,2,0:T(2,128)S(1)}, f32[1,2,3,768]{3,1,2,0:T(2,128)}, u32[]{:S(2)}) copy-start(f32[1,2,3,768]{3,1,2,0:T(2,128)} %copy.41) | copy-start | bytes 55300
  28.0 2.4 %copy-start.3 = (f32[1,2,3,768]{3,1,2,0:T(2,128)S(1)}, f32[1,2,3,768]{3,1,2,0:T(2,128)}, u32[]{:S(2)}) copy-start(f32[1,2,3,768]{3,1,2,0:T(2,128)} %copy.40) | copy-start | bytes 55300
  35.6 5.5 %copy-start = (bf16[1,2304,384]{1,2,0:T(8,128)(2,1)S(1)}, bf16[1,2304,384]{1,2,0:T(8,128)(2,1)}, u32[]{:S(2)}) copy-start(bf16[1,2304,384]{1,2,0:T(8,128)(2,1)} %copy.22) | copy-start | bytes 5308420
  41.1 3.5 %copy-start.1 = (bf16[1,2,2304,768]{2,3,1,0:T(8,128)(2,1)S(1)}, bf16[1,2,2304,768]{2,3,1,0:T(8,128)(2,1)}, u32[]{:S(2)}) copy-start(bf16[1,2,2304,768]{2,3,1,0:T(8,128)(2,1)} %pad_maximum_fusion) | copy-start | bytes 21233668
  50.4 0.7 copy-start.4
  125.4 55.5 %all-to-all-start = ((bf16[1,2,1536,384]{3,1,0,2:T(2,128)(2,1)}), bf16[1,2,1536,384]{3,1,0,2:T(2,128)(2,1)S(1)}, u32[]{:S(2)}, u32[]{:S(2)}) async-start(bf16[1,2,1536,384]{3,1,0,2:T(2,128)(2,1)} %copy.30), calls=%async_computation | async-start | bytes 4718592 | tf_op jit(solution)/shard_map/all_to_all | solution.py:140
  129.1 38.4 %all-reduce.3.cloned.1.call-start = ((), (), s32[]{:S(2)}) async-start(), calls=%async_computation.1 | async-start | bytes 1179648 | tf_op jit(solution)/shard_map/psum | solution.py:13
Sparse Core Ops, SparseCore 0:
  132.2 35.2 all-reduce.2
where the time goes:
time: 199 us
  local copies, waits for them, and re-layouts  51.9 us (26%)
  blocking collectives  49 us (25%)
  waiting for transfers between devices  48 us (24%)
  other arithmetic  20.4 us (10%)
  between operations  14.2 us (7%)
  matrix products  11.6 us (6%)
  starting transfers between devices  3.67 us (2%)
    psum x1, blocking collectives, body(): summed = lax.psum(partial_sums, 'space')  49 us
    psum x1, waiting for transfers between devices, spread(): return lax.psum(kept, axis)  36.8 us
    convert_element_type x1, local copies, waits for them, and re-layouts, propagate(): product.reshape(2, spin_count * vector_count, column_count)  12.6 us
    all_to_all x1, waiting for transfers between devices, body(): lax.all_to_all(propagated, 'space', split_axis=2, concat_axis=3, tiled=True)  11.2 us
    another operation x1, local copies, waits for them, and re-layouts, body(): jnp.stack([attach_source(lax.all_to_all(propagated, 'space', split_axis=2...  6.04 us
    dot_general x1, matrix products, elementals(): lax.dot_general(plain_vectors, phased, (((1,), (1,)), ((0,), (0,))), pref...  5.66 us
    concatenate x1, other arithmetic, elementals(): phased = jnp.concatenate([phased_real, phased_imaginary], axis=3)  5.5 us
    convert_element_type x1, other arithmetic, elementals(): (cos_rows * real_rows[:, None] + sin_rows * imaginary_rows[:, None]).asty...  5.22 us
  transfers between devices with their start and end apart: 2, of which 2 were waited for; matrix products, arithmetic and copies ran while one was open for 2% of the time, Pallas kernels for 0%

commit v1 on v0

--- a/solution.py
+++ b/solution.py
@@ -3,9 +3,13 @@
 import jax
 import jax.numpy as jnp
 from jax import lax
+from jax.experimental import pallas as pl
+from jax.experimental.pallas import tpu as pltpu
 from jax.sharding import PartitionSpec as P
 
+
 LSIDE = 64
+SPINS = 4
 
 
 def spread(value, axis, source):
@@ -112,7 +116,7 @@
     return product.reshape(2, row_count, spin_count * vector_count)
 
 
-def body(eigenvectors, perambulator, momenta, ratios, source_slice):
+def general_body(eigenvectors, perambulator, momenta, ratios, source_slice):
     slab_count = eigenvectors.shape[0]
     color_count = eigenvectors.shape[2]
     site_count = eigenvectors.shape[3]
@@ -133,14 +137,447 @@
     )
     chosen = spread(local_source, "tm", global_slice // slab_count)
     source_big = source_block(chosen)
-    propagated = jnp.stack([propagate(sink_matrices[0], perambulator[0])])
-    return jnp.stack(
-        [
-            attach_source(
-                lax.all_to_all(propagated, "space", split_axis=2, concat_axis=3, tiled=True)[0],
-                source_big,
+    results = []
+    for slab in range(slab_count):
+        propagated = propagate(sink_matrices[slab], perambulator[slab])[None]
+        turned = lax.all_to_all(propagated, "space", split_axis=2, concat_axis=3, tiled=True)
+        results.append(attach_source(turned[0], source_big))
+    return jnp.stack(results)
+
+
+HBM = pl.BlockSpec(memory_space=pltpu.MemorySpace.HBM)
+
+
+def pick_kernel(tau_hbm, out_hbm, buffer, in_sems, out_sems):
+    which = lax.axis_index("space") ^ 3
+    loads = [
+        pltpu.make_async_copy(tau_hbm.at[part, which], buffer.at[part], in_sems.at[part])
+        for part in range(2)
+    ]
+    stores = [
+        pltpu.make_async_copy(buffer.at[part], out_hbm.at[part], out_sems.at[part])
+        for part in range(2)
+    ]
+    for copy in loads:
+        copy.start()
+    for load, store in zip(loads, stores):
+        load.wait()
+        store.start()
+    for copy in stores:
+        copy.wait()
+
+
+def pick_block(tau):
+    _, _, n, columns = tau.shape
+    return pl.pallas_call(
+        pick_kernel,
+        in_specs=[HBM],
+        out_specs=HBM,
+        scratch_shapes=[
+            pltpu.VMEM((2, n, columns), tau.dtype),
+            pltpu.SemaphoreType.DMA((2,)),
+            pltpu.SemaphoreType.DMA((2,)),
+        ],
+        out_shape=jax.ShapeDtypeStruct((2, n, columns), tau.dtype),
+        name="pick",
+    )(tau)
+
+
+def elemental_kernel(
+    momenta,
+    ratios,
+    v_hbm,
+    tau_hbm,
+    rounded_a,
+    rounded_b,
+    full_a,
+    full_b,
+    by1,
+    by2,
+    vectors,
+    blocks,
+    table,
+    phased,
+    total,
+    sems,
+    in_sems,
+    out_sems,
+):
+    place = lax.axis_index("space")
+    colors = v_hbm.shape[1]
+    site_count = v_hbm.shape[2]
+    n = v_hbm.shape[3]
+    half = n // 2
+    loads = [
+        pltpu.make_async_copy(v_hbm.at[:, c], vectors.at[c], sems.at[c]) for c in range(colors)
+    ]
+    fetches = [
+        pltpu.make_async_copy(tau_hbm.at[:, place ^ r], blocks.at[r - 1], in_sems.at[r - 1])
+        for r in (1, 2)
+    ]
+    stores = [
+        pltpu.make_async_copy(blocks.at[i], out, out_sems.at[i]) for i, out in enumerate((by1, by2))
+    ]
+    for copy in loads + fetches:
+        copy.start()
+
+    row = lax.broadcasted_iota(jnp.int32, (8, 128), 0)
+    lane = lax.broadcasted_iota(jnp.int32, (8, 128), 1)
+    second = (row & 1) == 1
+    along = [jnp.where(second, momenta[1, a], momenta[0, a]) for a in range(3)]
+    shift = jnp.where((row & 2) == 2, LSIDE - LSIDE // 4, 0)
+    for tile in range(site_count // 128):
+        site = place * site_count + tile * 128 + lane
+        turn = (
+            along[0] * (site % LSIDE)
+            + along[1] * (site // LSIDE % LSIDE)
+            + along[2] * (site // (LSIDE * LSIDE))
+            + shift
+        )
+        turn = turn & (LSIDE - 1)
+        angle = turn.astype(jnp.float32) * (2.0 * math.pi / LSIDE)
+        table[pl.ds(tile * 128, 128), 0:8] = jnp.cos(angle).T
+
+    def phase(color, k):
+        slot = (2 * color + k) % 2
+        real = vectors[color, 0].astype(jnp.float32)
+        imag = vectors[color, 1].astype(jnp.float32)
+        c = table[:, k : k + 1]
+        s = table[:, k + 2 : k + 3]
+        phased[slot, :, 0:n] = (c * real + s * imag).astype(jnp.bfloat16)
+        phased[slot, :, n : 2 * n] = (c * imag - s * real).astype(jnp.bfloat16)
+
+    def multiply(color, k):
+        slot = (2 * color + k) % 2
+        cols = slice(2 * k * n, (2 * k + 2) * n)
+        for part in range(2):
+            product = lax.dot_general(
+                vectors[color, part],
+                phased[slot],
+                (((0,), (0,)), ((), ())),
+                preferred_element_type=jnp.float32,
             )
-        ]
+            rows = slice(part * n, (part + 1) * n)
+            if color == 0:
+                total[rows, cols] = product
+            else:
+                total[rows, cols] += product
+
+    before = None
+    for color in range(colors):
+        loads[color].wait()
+        for k in range(2):
+            phase(color, k)
+            if before is not None:
+                multiply(*before)
+            before = (color, k)
+        if color == 1:
+            for copy in fetches:
+                copy.wait()
+            for copy in stores:
+                copy.start()
+    multiply(*before)
+
+    normalizer = 1.0 / math.sqrt(colors * site_count * lax.axis_size("space") * n)
+    re = 0.0
+    im = 0.0
+    for k in range(2):
+        ratio = [jnp.full((8, 128), ratios[k, i], jnp.int32).astype(jnp.float32) for i in range(2)]
+        w = (ratio[0] / ratio[1] * normalizer)[0:1, 0:1]
+        zr = slice((2 * k) * n, (2 * k + 1) * n)
+        zi = slice((2 * k + 1) * n, (2 * k + 2) * n)
+        re += w * (total[0:n, zr] + total[n : 2 * n, zi])
+        im += w * (total[0:n, zi] - total[n : 2 * n, zr])
+    for part, value in enumerate((re, im)):
+        small = value.astype(jnp.bfloat16)
+        rounded_a[part] = small[:half]
+        rounded_b[part] = small[half:]
+        full_a[part] = value[:half]
+        full_b[part] = value[half:]
+    for copy in stores:
+        copy.wait()
+
+
+def elemental_sums(vectors, tau, momenta, ratios):
+    _, color_count, site_count, n = vectors.shape
+    half = n // 2
+    rows = pl.BlockSpec((2, half, n), lambda i, *_: (0, 0, 0))
+    return pl.pallas_call(
+        elemental_kernel,
+        grid_spec=pltpu.PrefetchScalarGridSpec(
+            num_scalar_prefetch=2,
+            grid=(1,),
+            in_specs=[HBM, HBM],
+            out_specs=[rows] * 4 + [HBM] * 2,
+            scratch_shapes=[
+                pltpu.VMEM((color_count, 2, site_count, n), jnp.bfloat16),
+                pltpu.VMEM((2, 2, n, n), jnp.bfloat16),
+                pltpu.VMEM((site_count, 128), jnp.float32),
+                pltpu.VMEM((2, site_count, 2 * n), jnp.bfloat16),
+                pltpu.VMEM((2 * n, 4 * n), jnp.float32),
+                pltpu.SemaphoreType.DMA((color_count,)),
+                pltpu.SemaphoreType.DMA((2,)),
+                pltpu.SemaphoreType.DMA((2,)),
+            ],
+        ),
+        out_shape=[
+            jax.ShapeDtypeStruct((2, rows_of, n), dtype)
+            for rows_of, dtype in (
+                (half, jnp.bfloat16),
+                (half, jnp.bfloat16),
+                (half, jnp.float32),
+                (half, jnp.float32),
+                (n, jnp.bfloat16),
+                (n, jnp.bfloat16),
+            )
+        ],
+        compiler_params=pltpu.CompilerParams(vmem_limit_bytes=40 * 1024 * 1024),
+        name="elementals",
+    )(momenta, ratios, vectors, tau)
+
+
+def complex_rows(real, imag):
+    upper = jnp.concatenate([real, imag], axis=1)
+    lower = jnp.concatenate([-imag, real], axis=1)
+    return jnp.concatenate([upper, lower], axis=0)
+
+
+def sandwich(sink, tau_re, tau_im, source):
+    prop = jnp.dot(sink, complex_rows(tau_re, tau_im), preferred_element_type=jnp.float32)
+    return lax.dot_general(
+        prop.astype(jnp.bfloat16),
+        source,
+        (((1,), (1,)), ((), ())),
+        preferred_element_type=jnp.float32,
+    )
+
+
+def copy_if(flag, first, second, target, sem):
+    @pl.when(flag == 1)
+    def _():
+        pltpu.make_async_copy(first, target, sem).start()
+
+    @pl.when(flag != 1)
+    def _():
+        pltpu.make_async_copy(second, target, sem).start()
+
+
+def is_inner(place):
+    return jnp.where((place == 1) | (place == 2), 1, 0)
+
+
+def three_kernel(source_slice, *refs):
+    (sum_a, sum_b, out_a, out_b, here_a, here_b, far_a, far_b, beside_a, beside_b) = refs[:10]
+    tau_hbm, got_n, got_b, got_c = refs[10:14]
+    out_hbm, sink_out, source_out = refs[14:17]
+    sink, source, blocks, staged, sink_sems, source_sems, block_sems, out_sems = refs[17:]
+    n = sink_out.shape[0]
+    half = n // 2
+    quarter = n // 4
+    place = lax.axis_index("space")
+    time = lax.axis_index("tm")
+    inner = is_inner(place)
+    same = jnp.where(source_slice[0] % lax.axis_size("tm") // 2 == time // 2, 1, 0)
+    odd = time % 2
+
+    for i, (mine, got) in enumerate(((sum_a, out_a), (sum_b, out_b))):
+        copy_if(inner, mine, got, sink.at[:, pl.ds(i * half, half)], sink_sems.at[i])
+    pltpu.make_async_copy(tau_hbm.at[:, place], blocks.at[0], block_sems.at[0]).start()
+    pltpu.make_async_copy(got_n, blocks.at[1], block_sems.at[1]).start()
+    for i, (here, far, beside) in enumerate(
+        ((here_a, far_a, beside_a), (here_b, far_b, beside_b))
+    ):
+        rows = source.at[:, pl.ds(i * half, half)]
+
+        @pl.when(same == 1)
+        def _():
+            first, second = pl.ds(0, quarter), pl.ds(quarter, quarter)
+            pltpu.make_async_copy(here.at[:, first], rows.at[:, first], source_sems.at[2 * i]).start()
+            pltpu.make_async_copy(
+                here.at[:, second], rows.at[:, second], source_sems.at[2 * i + 1]
+            ).start()
+
+        @pl.when(same != 1)
+        def _():
+            mine = pl.multiple_of(odd * quarter, 16)
+            other = pl.multiple_of((1 - odd) * quarter, 16)
+            pltpu.make_async_copy(
+                far, rows.at[:, pl.ds(mine, quarter)], source_sems.at[2 * i]
+            ).start()
+            pltpu.make_async_copy(
+                beside, rows.at[:, pl.ds(other, quarter)], source_sems.at[2 * i + 1]
+            ).start()
+
+    copy_if(inner, got_b, got_c, blocks.at[2], block_sems.at[2])
+
+    for i, got in enumerate((out_a, out_b)):
+        pltpu.make_async_copy(got, sink.at[:, pl.ds(i * half, half)], sink_sems.at[i]).wait()
+    sink_rows = jnp.concatenate([sink[0], sink[1]], axis=1)
+    sink_out[...] = sink_rows
+    for i in range(2):
+        for q in range(2):
+            pltpu.make_async_copy(
+                far_a, source.at[:, pl.ds(0, quarter)], source_sems.at[2 * i + q]
+            ).wait()
+    source_rows = complex_rows(source[0], source[1])
+    source_out[...] = source_rows
+
+    stores = []
+    for i in range(3):
+        pltpu.make_async_copy(got_n, blocks.at[i], block_sems.at[i]).wait()
+        product = sandwich(sink_rows, blocks[i, 0], blocks[i, 1], source_rows)
+        staged[i, 0] = product[:, :n]
+        staged[i, 1] = product[:, n:]
+        column = pl.multiple_of((place ^ i) * n, 128)
+        store = pltpu.make_async_copy(
+            staged.at[i], out_hbm.at[0, :, :, pl.ds(column, n)], out_sems.at[i]
+        )
+        store.start()
+        stores.append(store)
+    for store in stores:
+        store.wait()
+
+
+def three_blocks(source_slice, pieces, tau, got, spins):
+    n = tau.shape[2]
+    return pl.pallas_call(
+        three_kernel,
+        grid_spec=pltpu.PrefetchScalarGridSpec(
+            num_scalar_prefetch=1,
+            grid=(1,),
+            in_specs=[HBM] * 14,
+            out_specs=[
+                HBM,
+                pl.BlockSpec((n, 2 * n), lambda i, *_: (0, 0)),
+                pl.BlockSpec((2 * n, 2 * n), lambda i, *_: (0, 0)),
+            ],
+            scratch_shapes=[
+                pltpu.VMEM((2, n, n), jnp.bfloat16),
+                pltpu.VMEM((2, n, n), jnp.bfloat16),
+                pltpu.VMEM((3, 2, n, n), jnp.bfloat16),
+                pltpu.VMEM((3, 2, n, n), jnp.float32),
+                pltpu.SemaphoreType.DMA((2,)),
+                pltpu.SemaphoreType.DMA((4,)),
+                pltpu.SemaphoreType.DMA((3,)),
+                pltpu.SemaphoreType.DMA((3,)),
+            ],
+        ),
+        out_shape=[
+            jax.ShapeDtypeStruct((1, 2, n, spins * n), jnp.float32),
+            jax.ShapeDtypeStruct((n, 2 * n), jnp.bfloat16),
+            jax.ShapeDtypeStruct((2 * n, 2 * n), jnp.bfloat16),
+        ],
+        compiler_params=pltpu.CompilerParams(vmem_limit_bytes=40 * 1024 * 1024),
+        name="three",
+    )(source_slice, *pieces, tau, *got)
+
+
+def last_kernel(sink, source, got_a, got_d, _, out_hbm, block, staged, sem, out_sem):
+    n = sink.shape[0]
+    place = lax.axis_index("space")
+    copy_if(is_inner(place), got_a, got_d, block, sem)
+    pltpu.make_async_copy(got_a, block, sem).wait()
+    product = sandwich(sink[...], block[0], block[1], source[...])
+    staged[0] = product[:, :n]
+    staged[1] = product[:, n:]
+    column = pl.multiple_of((place ^ 3) * n, 128)
+    store = pltpu.make_async_copy(staged, out_hbm.at[0, :, :, pl.ds(column, n)], out_sem)
+    store.start()
+    store.wait()
+
+
+def last_block(sink, source, got_a, got_d, out):
+    n = sink.shape[0]
+    return pl.pallas_call(
+        last_kernel,
+        grid=(1,),
+        in_specs=[
+            pl.BlockSpec((n, 2 * n), lambda i: (0, 0)),
+            pl.BlockSpec((2 * n, 2 * n), lambda i: (0, 0)),
+            HBM,
+            HBM,
+            HBM,
+        ],
+        out_specs=HBM,
+        scratch_shapes=[
+            pltpu.VMEM((2, n, n), jnp.bfloat16),
+            pltpu.VMEM((2, n, n), jnp.float32),
+            pltpu.SemaphoreType.DMA,
+            pltpu.SemaphoreType.DMA,
+        ],
+        out_shape=jax.ShapeDtypeStruct(out.shape, out.dtype),
+        input_output_aliases={4: 0},
+        compiler_params=pltpu.CompilerParams(vmem_limit_bytes=40 * 1024 * 1024),
+        name="last",
+    )(sink, source, got_a, got_d, out)
+
+
+def block_body(eigenvectors, perambulator, momenta, ratios, source_slice):
+    return ordered_body(eigenvectors, perambulator, momenta, ratios, source_slice)
+
+
+def ordered_body(eigenvectors, perambulator, momenta, ratios, source_slice):
+    n = eigenvectors.shape[4]
+    quarter = n // 4
+    spins = lax.axis_size("space")
+    j = lax.axis_index("space")
+    inner = (j == 1) | (j == 2)
+    odd = lax.axis_index("tm") % 2
+    tau = perambulator[0].reshape(2, spins, n, n)
+
+    def move(value, pairs, axis="space"):
+        return lax.ppermute(value, axis, pairs)
+
+    middle = [(1, 2), (2, 1)]
+    ends = [(0, 3), (3, 0)]
+    inward = [(0, 1), (3, 2)]
+    outward = [(1, 0), (2, 3)]
+    skip_in = [(0, 2), (3, 1)]
+    skip_out = [(1, 3), (2, 0)]
+    core = [(0, 1), (1, 0), (2, 3), (3, 2)]
+    chip = [(0, 2), (2, 0), (1, 3), (3, 1)]
+
+    by3 = pick_block(tau)
+    got_a = move(by3, middle)
+    rounded_a, rounded_b, full_a, full_b, by1, by2 = elemental_sums(
+        eigenvectors[0], tau, momenta, ratios
+    )
+    got_n = move(by1, inward + outward)
+    got_c = move(by2, skip_out)
+    got_b = move(by2, skip_in)
+    got_d = move(by3, ends)
+
+    pieces = []
+    for rounded, full in ((rounded_a, full_a), (rounded_b, full_b)):
+        inside = move(rounded, inward)
+        pair = full + inside.astype(jnp.float32)
+        across = move(pair.astype(jnp.bfloat16), middle)
+        summed = (pair + across.astype(jnp.float32)).astype(jnp.bfloat16)
+        outside = move(summed, outward)
+        sink = jnp.where(inner, summed, outside)
+        partner = move(sink, core, "tm")
+        here = jnp.where(source_slice[0] % 2 == odd, sink, partner)
+        mine = lax.dynamic_slice_in_dim(here, odd * quarter, quarter, 1)
+        far = move(mine, chip, "tm")
+        beside = move(far, core, "tm")
+        pieces.append((summed, outside, here, far, beside))
+    pieces = [piece for pair in zip(*pieces) for piece in pair]
+
+    out, sink, source = three_blocks(source_slice, pieces, tau, (got_n, got_b, got_c), spins)
+    return last_block(sink, source, got_a, got_d, out)
+
+
+def fits(mesh, eigenvectors, perambulator):
+    n = eigenvectors.shape[4]
+    space = mesh.shape["space"]
+    return (
+        eigenvectors.shape[0] == mesh.shape["cfg"] * mesh.shape["tm"]
+        and space == SPINS
+        and mesh.shape["tm"] == 4
+        and perambulator.shape[2] == space * n
+        and perambulator.shape[3] == space * n
+        and eigenvectors.shape[3] % (128 * space) == 0
+        and n % 128 == 0
     )
 
 
@@ -152,10 +589,19 @@
         P(),
         P(),
     )
-    return jax.shard_map(
-        body,
-        mesh=mesh,
-        in_specs=placed,
-        out_specs=P(("cfg", "tm"), None, "space", None),
-        check_vma=False,
-    )
+
+    def mapped(body):
+        return jax.shard_map(
+            body,
+            mesh=mesh,
+            in_specs=placed,
+            out_specs=P(("cfg", "tm"), None, "space", None),
+            check_vma=False,
+        )
+
+    def program(*arrays):
+        if not fits(mesh, arrays[0], arrays[1]):
+            return mapped(general_body)(*arrays)
+        return mapped(block_body)(*arrays)
+
+    return program

time: 199 us -> 126 us (0.63)
  blocking collectives: 49 us -> 0 us
  local copies, waits for them, and re-layouts: 51.9 us -> 5.09 us
  waiting for transfers between devices: 48 us -> 70.8 us
  starting transfers between devices: 3.67 us -> 25.3 us
  Pallas kernels: 0 us -> 19.6 us
  other arithmetic: 20.4 us -> 3.84 us
  between operations: 14.2 us -> 1.1 us
  matrix products: 11.6 us -> 0 us
    ppermute x0 -> x17, waiting for transfers between devices: none -> 70.8 us  [move(): return lax.ppermute(value, axis, pairs)]
    psum x1 -> x0, blocking collectives: 49 us -> none  [body(): summed = lax.psum(partial_sums, 'space')]
    psum x1 -> x0, waiting for transfers between devices: 36.8 us -> none  [spread(): return lax.psum(kept, axis)]
    ppermute x0 -> x17, starting transfers between devices: none -> 25.3 us  [move(): return lax.ppermute(value, axis, pairs)]
    convert_element_type x3 -> x0, local copies, waits for them, and re-layouts: 22.9 us -> none  [the longest x1 12.6 us: propagate(): product.reshape(2, spin_count * vector_count, column_count)]
    pallas_call x0 -> x4, Pallas kernels: none -> 19.6 us  [the longest x1 8.66 us: elemental_sums(): pl.pallas_call(elemental_kernel, grid_spec=pltpu.PrefetchScalarGridSpec(n...]
    another operation x4 -> x0, local copies, waits for them, and re-layouts: 14.3 us -> none  [the longest x1 6.04 us: body(): jnp.stack([attach_source(lax.all_to_all(propagated, 'space', split_axis=2...]
    dot_general x3 -> x0, matrix products: 11.6 us -> none  [the longest x1 5.66 us: elementals(): lax.dot_general(plain_vectors, phased, (((1,), (1,)), ((0,), (0,))), pref...]
  transfers between devices with their start and end apart: 2 -> 17, of which waited for: 2 -> 8; matrix products, arithmetic and copies ran while one was open for 2% -> 3% of each run, Pallas kernels for 0% -> 6%
where the time goes in v1:
time: 126 us
  waiting for transfers between devices  70.8 us (56%)
  starting transfers between devices  25.3 us (20%)
  Pallas kernels  19.6 us (16%)
  local copies, waits for them, and re-layouts  5.09 us (4%)
  other arithmetic  3.84 us (3%)
    ppermute x17, waiting for transfers between devices, move(): return lax.ppermute(value, axis, pairs)  70.8 us
    ppermute x17, starting transfers between devices, move(): return lax.ppermute(value, axis, pairs)  25.3 us
    pallas_call x1, Pallas kernels, elemental_sums(): pl.pallas_call(elemental_kernel, grid_spec=pltpu.PrefetchScalarGridSpec(n...  8.66 us
    pallas_call x1, Pallas kernels, three_blocks(): pl.pallas_call(three_kernel, grid_spec=pltpu.PrefetchScalarGridSpec(num_s...  5.85 us
    unnamed x14, local copies, waits for them, and re-layouts  5.04 us
    pallas_call x1, Pallas kernels, last_block(): pl.pallas_call(last_kernel, grid=(1,), in_specs=[pl.BlockSpec((n, 2 * n),...  3.31 us
  transfers between devices with their start and end apart: 17, of which 8 were waited for; matrix products, arithmetic and copies ran while one was open for 3% of the time, Pallas kernels for 6%

profile of v1, /device:TPU:0, one launch (start us, length us, event | category | flops | bytes accessed | tf_op | source)
XLA Modules:
  0.0 125.8 jit_solution(18101376913903631124)
XLA Ops:
  0.0 1.7 %copy-done = bf16[1,2,1536,384]{3,2,1,0:T(8,128)(2,1)S(1)} copy-done((bf16[1,2,1536,384]{3,2,1,0:T(8,128)(2,1)S(1)}, bf16[1,2,1536,384]{3,2,1,0:T(8,128)(2,1)}, u32[]{:S(2)}) %copy-start) | copy-done | bytes 2359320
  1.7 2.0 %copy-done.2 = bf16[1,2,3,768,384]{4,3,2,1,0:T(8,128)(2,1)S(1)} copy-done((bf16[1,2,3,768,384]{4,3,2,1,0:T(8,128)(2,1)S(1)}, bf16[1,2,3,768,384]{4,3,2,1,0:T(8,128)(2,1)}, u32[]{:S(2)}) %copy-start.2) | copy-done | bytes 3538968
  3.7 0.7 copy-done.3
  4.3 0.7 copy-done.4
  5.0 8.7 %elementals.1 = (bf16[2,192,384]{2,1,0:T(8,128)(2,1)S(1)}, bf16[2,192,384]{2,1,0:T(8,128)(2,1)S(1)}, f32[2,192,384]{2,1,0:T(8,128)S(1)}, f32[2,192,384]{2,1,0:T(...) custom-call(s32[2,3]{1,0:T(2,128)S(1)} %copy-done.3, s32[2,2]{1,0:T(2,128)S(1)} %copy-done.4, ...), custom_call_target="tpu_custom_call" | custom-call | tf_op jit(solution)/shard_map/elementals/pallas_call | solution.py:305
  13.7 5.0 %collective-permute-start = (bf16[2,192,384]{2,1,0:T(8,128)(2,1)S(1)}, bf16[2,192,384]{2,1,0:T(8,128)(2,1)S(1)}, u32[]{:S(2)}, u32[]{:S(2)}) collective-permute-start(bf16[2,192,384]{2,1,0:T(8,128)(2,1)S(1)} %get-tuple-element.15), channel_id=1, source_target_pairs={{0,4},{12,8},{1,5},{13,9},{2,6},{14,10},{3,7},{15,11},{16,20},{28,... | collective-permute-start | bytes 884744 | tf_op jit(solution)/shard_map/ppermute | solution.py:529
  18.7 1.3 %collective-permute-start.2 = (bf16[2,192,384]{2,1,0:T(8,128)(2,1)S(1)}, bf16[2,192,384]{2,1,0:T(8,128)(2,1)S(1)}, u32[]{:S(2)}, u32[]{:S(2)}) collective-permute-start(bf16[2,192,384]{2,1,0:T(8,128)(2,1)S(1)} %get-tuple-element.17), channel_id=1, source_target_pairs={{0,4},{12,8},{1,5},{13,9},{2,6},{14,10},{3,7},{15,11},{16,20},{28,... | collective-permute-start | bytes 884744 | tf_op jit(solution)/shard_map/ppermute | solution.py:529
  20.0 6.0 %collective-permute-done = bf16[2,192,384]{2,1,0:T(8,128)(2,1)S(1)} collective-permute-done((bf16[2,192,384]{2,1,0:T(8,128)(2,1)S(1)}, bf16[2,192,384]{2,1,0:T(8,128)(2,1)S(1)}, u32[]{:S(2)}, u32[]{:S(2)}) %collective-permute-start) | collective-permute-done | bytes 294944 | tf_op jit(solution)/shard_map/ppermute | solution.py:529
  26.1 0.7 collective-permute-start.1
  26.8 4.4 %collective-permute-done.2 = bf16[2,192,384]{2,1,0:T(8,128)(2,1)S(1)} collective-permute-done((bf16[2,192,384]{2,1,0:T(8,128)(2,1)S(1)}, bf16[2,192,384]{2,1,0:T(8,128)(2,1)S(1)}, u32[]{:S(2)}, u32[]{:S(2)}) %collective-permute-start.2) | collective-permute-done | bytes 294944 | tf_op jit(solution)/shard_map/ppermute | solution.py:529
  31.3 0.7 collective-permute-start.3
  32.1 1.3 %collective-permute-start.4 = (bf16[2,192,384]{2,1,0:T(8,128)(2,1)S(1)}, bf16[2,192,384]{2,1,0:T(8,128)(2,1)S(1)}, u32[]{:S(2)}, u32[]{:S(2)}) collective-permute-start(bf16[2,192,384]{2,1,0:T(8,128)(2,1)S(1)} %add_convert_fusion.1.refs_0_), channel_id=1, source_target_pairs={{4,0},{8,12},{5,1},{9,13},{6,2},{10,14},{7,3},{11,15},{20,16},{24,... | collective-permute-start | bytes 884744 | tf_op jit(solution)/shard_map/ppermute | solution.py:529
  33.5 1.3 %collective-permute-start.5 = (bf16[2,192,384]{2,1,0:T(8,128)(2,1)S(1)}, bf16[2,192,384]{2,1,0:T(8,128)(2,1)S(1)}, u32[]{:S(2)}, u32[]{:S(2)}) collective-permute-start(bf16[2,192,384]{2,1,0:T(8,128)(2,1)S(1)} %add_convert_fusion.refs_1_), channel_id=1, source_target_pairs={{4,0},{8,12},{5,1},{9,13},{6,2},{10,14},{7,3},{11,15},{20,16},{24,... | collective-permute-start | bytes 884744 | tf_op jit(solution)/shard_map/ppermute | solution.py:529
  34.9 10.3 %collective-permute-done.4.refs_2_ = bf16[2,192,384]{2,1,0:T(8,128)(2,1)S(1)} collective-permute-done((bf16[2,192,384]{2,1,0:T(8,128)(2,1)S(1)}, bf16[2,192,384]{2,1,0:T(8,128)(2,1)S(1)}, u32[]{:S(2)}, u32[]{:S(2)}) %collective-permute-start.4) | collective-permute-done | bytes 294944 | tf_op jit(solution)/shard_map/ppermute | solution.py:529
  45.1 0.8 broadcast_select_fusion.1
  45.9 5.0 %collective-permute-done.5.refs_3_ = bf16[2,192,384]{2,1,0:T(8,128)(2,1)S(1)} collective-permute-done((bf16[2,192,384]{2,1,0:T(8,128)(2,1)S(1)}, bf16[2,192,384]{2,1,0:T(8,128)(2,1)S(1)}, u32[]{:S(2)}, u32[]{:S(2)}) %collective-permute-start.5) | collective-permute-done | bytes 294944 | tf_op jit(solution)/shard_map/ppermute | solution.py:529
  50.9 0.8 broadcast_select_fusion
  51.6 1.8 %pick.1 = bf16[2,384,384]{2,1,0:T(8,128)(2,1)} custom-call(bf16[2,4,384,384]{3,2,1,0:T(8,128)(2,1)} %bitcast.6), custom_call_target="tpu_custom_call" | custom-call | tf_op jit(solution)/shard_map/pick/pallas_call | solution.py:172
  53.4 3.8 %collective-permute-start.16 = (bf16[2,384,384]{2,1,0:T(8,128)(2,1)}, bf16[2,384,384]{2,1,0:T(8,128)(2,1)}, u32[]{:S(2)}, u32[]{:S(2)}) collective-permute-start(bf16[2,384,384]{2,1,0:T(8,128)(2,1)} %pick.1), channel_id=1, source_target_pairs={{0,12},{12,0},{1,13},{13,1},{2,14},{14,2},{3,15},{15,3},{16,28},{2... | collective-permute-start | bytes 1769480 | tf_op jit(solution)/shard_map/ppermute | solution.py:529
  57.2 1.5 %collective-permute-start.15 = (bf16[2,384,384]{2,1,0:T(8,128)(2,1)}, bf16[2,384,384]{2,1,0:T(8,128)(2,1)}, u32[]{:S(2)}, u32[]{:S(2)}) collective-permute-start(bf16[2,384,384]{2,1,0:T(8,128)(2,1)} %pick.1), channel_id=1, source_target_pairs={{4,8},{8,4},{5,9},{9,5},{6,10},{10,6},{7,11},{11,7},{20,24},{24,20... | collective-permute-start | bytes 1769480 | tf_op jit(solution)/shard_map/ppermute | solution.py:529
  59.4 1.3 %collective-permute-start.14 = (bf16[2,384,384]{2,1,0:T(8,128)(2,1)}, bf16[2,384,384]{2,1,0:T(8,128)(2,1)S(1)}, u32[]{:S(2)}, u32[]{:S(2)}) collective-permute-start(bf16[2,384,384]{2,1,0:T(8,128)(2,1)} %copy-done.5), channel_id=1, source_target_pairs={{4,12},{8,0},{5,13},{9,1},{6,14},{10,2},{7,15},{11,3},{20,28},{24,... | collective-permute-start | bytes 1769480 | tf_op jit(solution)/shard_map/ppermute | solution.py:529
  60.7 1.0 broadcast_select_fusion.3.refs_4_
  61.7 5.5 %collective-permute-start.13 = (bf16[2,384,384]{2,1,0:T(8,128)(2,1)}, bf16[2,384,384]{2,1,0:T(8,128)(2,1)S(1)}, u32[]{:S(2)}, u32[]{:S(2)}) collective-permute-start(bf16[2,384,384]{2,1,0:T(8,128)(2,1)} %copy-done.5), channel_id=1, source_target_pairs={{0,8},{12,4},{1,9},{13,5},{2,10},{14,6},{3,11},{15,7},{16,24},{28,... | collective-permute-start | bytes 1769480 | tf_op jit(solution)/shard_map/ppermute | solution.py:529
  67.2 1.0 broadcast_select_fusion.2.refs_5_
  68.3 19.1 %collective-permute-done.12.refs_11_ = bf16[2,384,384]{2,1,0:T(8,128)(2,1)} collective-permute-done((bf16[2,384,384]{2,1,0:T(8,128)(2,1)}, bf16[2,384,384]{2,1,0:T(8,128)(2,1)}, u32[]{:S(2)}, u32[]{:S(2)}) %collective-permute-start.12) | collective-permute-done | bytes 589856 | tf_op jit(solution)/shard_map/ppermute | solution.py:529
  87.5 1.5 %collective-permute-start.8 = (bf16[2,96,384]{2,1,0:T(8,128)(2,1)S(1)}, bf16[2,96,384]{2,1,0:T(8,128)(2,1)S(1)}, u32[]{:S(2)}, u32[]{:S(2)}) collective-permute-start(bf16[2,96,384]{2,1,0:T(8,128)(2,1)S(1)} %constant_dynamic-slice_fusion.1), channel_id=1, source_target_pairs={{0,2},{2,0},{1,3},{3,1},{4,6},{6,4},{5,7},{7,5},{8,10},{10,8},{9,1... | collective-permute-start | bytes 442376 | tf_op jit(solution)/shard_map/ppermute | solution.py:529
  89.0 20.7 %collective-permute-done.14.refs_13_ = bf16[2,384,384]{2,1,0:T(8,128)(2,1)S(1)} collective-permute-done((bf16[2,384,384]{2,1,0:T(8,128)(2,1)}, bf16[2,384,384]{2,1,0:T(8,128)(2,1)S(1)}, u32[]{:S(2)}, u32[]{:S(2)}) %collective-permute-start.14) | collective-permute-done | bytes 589856 | tf_op jit(solution)/shard_map/ppermute | solution.py:529
  109.7 1.5 %collective-permute-start.9 = (bf16[2,96,384]{2,1,0:T(8,128)(2,1)S(1)}, bf16[2,96,384]{2,1,0:T(8,128)(2,1)S(1)}, u32[]{:S(2)}, u32[]{:S(2)}) collective-permute-start(bf16[2,96,384]{2,1,0:T(8,128)(2,1)S(1)} %constant_dynamic-slice_fusion), channel_id=1, source_target_pairs={{0,2},{2,0},{1,3},{3,1},{4,6},{6,4},{5,7},{7,5},{8,10},{10,8},{9,1... | collective-permute-start | bytes 442376 | tf_op jit(solution)/shard_map/ppermute | solution.py:529
  111.2 3.9 %collective-permute-done.9.refs_7_ = bf16[2,96,384]{2,1,0:T(8,128)(2,1)S(1)} collective-permute-done((bf16[2,96,384]{2,1,0:T(8,128)(2,1)S(1)}, bf16[2,96,384]{2,1,0:T(8,128)(2,1)S(1)}, u32[]{:S(2)}, u32[]{:S(2)}) %collective-permute-start.9) | collective-permute-done | bytes 147488 | tf_op jit(solution)/shard_map/ppermute | solution.py:529
  115.1 1.4 %collective-permute-done.11.refs_9_ = bf16[2,96,384]{2,1,0:T(8,128)(2,1)S(1)} collective-permute-done((bf16[2,96,384]{2,1,0:T(8,128)(2,1)S(1)}, bf16[2,96,384]{2,1,0:T(8,128)(2,1)S(1)}, u32[]{:S(2)}, u32[]{:S(2)}) %collective-permute-start.11) | collective-permute-done | bytes 147488 | tf_op jit(solution)/shard_map/ppermute | solution.py:529
  116.5 5.8 %three.1 = (f32[1,2,384,1536]{3,2,1,0:T(8,128)}, bf16[384,768]{1,0:T(8,128)(2,1)S(1)}, bf16[768,768]{1,0:T(8,128)(2,1)S(1)}) custom-call(s32[1]{0:T(128)} %copy.8.source_slice, bf16[2,192,384]{2,1,0:T(8,128)(2,1)S(1)} %add_convert_fusion.1.refs_0_, bf16[2,192,384]{2,1,0:T(8,128)(2,1)S(1)} %add_convert_fusion.refs_1_, ...), custom_call_target="tpu_custom_call" | custom-call | tf_op jit(solution)/shard_map/three/pallas_call | solution.py:443
  122.3 3.3 %last.1 = f32[1,2,384,1536]{3,2,1,0:T(8,128)} custom-call(bf16[384,768]{1,0:T(8,128)(2,1)S(1)} %get-tuple-element.20.sink, bf16[768,768]{1,0:T(8,128)(2,1)S(1)} %get-tuple-element.21.source, bf16[2,384,384]{2,1,0:T(8,128)(2,1)} %collective-permute-done.15.got_a, bf16[2,384,384]{2,1,0:T(8,128)(2,1)} %collective-permute-done.16.got_d, ...), custom_call_target="tpu_custom_call", output_to_operand_aliasing={{}: (4, {})} | custom-call | tf_op jit(solution)/shard_map/last/pallas_call | solution.py:491
  (30 shorter events, 0.4 us)
Async XLA Ops:
  0.0 1.7 %copy-start = (bf16[1,2,1536,384]{3,2,1,0:T(8,128)(2,1)S(1)}, bf16[1,2,1536,384]{3,2,1,0:T(8,128)(2,1)}, u32[]{:S(2)}) copy-start(bf16[1,2,1536,384]{3,2,1,0:T(8,128)(2,1)} %param.6) | copy-start | bytes 7077892
  1.7 2.0 %copy-start.2 = (bf16[1,2,3,768,384]{4,3,2,1,0:T(8,128)(2,1)S(1)}, bf16[1,2,3,768,384]{4,3,2,1,0:T(8,128)(2,1)}, u32[]{:S(2)}) copy-start(bf16[1,2,3,768,384]{4,3,2,1,0:T(8,128)(2,1)} %param.5) | copy-start | bytes 10616836
  3.7 0.7 copy-start.3
  4.3 0.7 copy-start.4
  13.7 21.1 %copy-start.5 = (bf16[2,384,384]{2,1,0:T(8,128)(2,1)}, bf16[2,384,384]{2,1,0:T(8,128)(2,1)S(1)}, u32[]{:S(2)}) copy-start(bf16[2,384,384]{2,1,0:T(8,128)(2,1)S(1)} %get-tuple-element.19) | copy-start | bytes 1769476
  13.7 21.1 %copy-start.6 = (bf16[2,384,384]{2,1,0:T(8,128)(2,1)}, bf16[2,384,384]{2,1,0:T(8,128)(2,1)S(1)}, u32[]{:S(2)}) copy-start(bf16[2,384,384]{2,1,0:T(8,128)(2,1)S(1)} %get-tuple-element.18) | copy-start | bytes 1769476
  13.7 12.3 %collective-permute-start = (bf16[2,192,384]{2,1,0:T(8,128)(2,1)S(1)}, bf16[2,192,384]{2,1,0:T(8,128)(2,1)S(1)}, u32[]{:S(2)}, u32[]{:S(2)}) collective-permute-start(bf16[2,192,384]{2,1,0:T(8,128)(2,1)S(1)} %get-tuple-element.15), channel_id=1, source_target_pairs={{0,4},{12,8},{1,5},{13,9},{2,6},{14,10},{3,7},{15,11},{16,20},{28,... | collective-permute-start | bytes 884744 | tf_op jit(solution)/shard_map/ppermute | solution.py:529
  18.7 12.6 %collective-permute-start.2 = (bf16[2,192,384]{2,1,0:T(8,128)(2,1)S(1)}, bf16[2,192,384]{2,1,0:T(8,128)(2,1)S(1)}, u32[]{:S(2)}, u32[]{:S(2)}) collective-permute-start(bf16[2,192,384]{2,1,0:T(8,128)(2,1)S(1)} %get-tuple-element.17), channel_id=1, source_target_pairs={{0,4},{12,8},{1,5},{13,9},{2,6},{14,10},{3,7},{15,11},{16,20},{28,... | collective-permute-start | bytes 884744 | tf_op jit(solution)/shard_map/ppermute | solution.py:529
  26.1 5.9 %collective-permute-start.1 = (bf16[2,192,384]{2,1,0:T(8,128)(2,1)S(1)}, bf16[2,192,384]{2,1,0:T(8,128)(2,1)S(1)}, u32[]{:S(2)}, u32[]{:S(2)}) collective-permute-start(bf16[2,192,384]{2,1,0:T(8,128)(2,1)S(1)} %fusion), channel_id=1, source_target_pairs={{4,8},{8,4},{5,9},{9,5},{6,10},{10,6},{7,11},{11,7},{20,24},{24,20... | collective-permute-start | bytes 884744 | tf_op jit(solution)/shard_map/ppermute | solution.py:529
  31.3 2.1 %collective-permute-start.3 = (bf16[2,192,384]{2,1,0:T(8,128)(2,1)S(1)}, bf16[2,192,384]{2,1,0:T(8,128)(2,1)S(1)}, u32[]{:S(2)}, u32[]{:S(2)}) collective-permute-start(bf16[2,192,384]{2,1,0:T(8,128)(2,1)S(1)} %fusion.1), channel_id=1, source_target_pairs={{4,8},{8,4},{5,9},{9,5},{6,10},{10,6},{7,11},{11,7},{20,24},{24,20... | collective-permute-start | bytes 884744 | tf_op jit(solution)/shard_map/ppermute | solution.py:529
  32.1 13.0 %collective-permute-start.4 = (bf16[2,192,384]{2,1,0:T(8,128)(2,1)S(1)}, bf16[2,192,384]{2,1,0:T(8,128)(2,1)S(1)}, u32[]{:S(2)}, u32[]{:S(2)}) collective-permute-start(bf16[2,192,384]{2,1,0:T(8,128)(2,1)S(1)} %add_convert_fusion.1.refs_0_), channel_id=1, source_target_pairs={{4,0},{8,12},{5,1},{9,13},{6,2},{10,14},{7,3},{11,15},{20,16},{24,... | collective-permute-start | bytes 884744 | tf_op jit(solution)/shard_map/ppermute | solution.py:529
  33.5 17.3 %collective-permute-start.5 = (bf16[2,192,384]{2,1,0:T(8,128)(2,1)S(1)}, bf16[2,192,384]{2,1,0:T(8,128)(2,1)S(1)}, u32[]{:S(2)}, u32[]{:S(2)}) collective-permute-start(bf16[2,192,384]{2,1,0:T(8,128)(2,1)S(1)} %add_convert_fusion.refs_1_), channel_id=1, source_target_pairs={{4,0},{8,12},{5,1},{9,13},{6,2},{10,14},{7,3},{11,15},{20,16},{24,... | collective-permute-start | bytes 884744 | tf_op jit(solution)/shard_map/ppermute | solution.py:529
  34.9 81.6 %copy-start.1 = (bf16[1,2,1536,384]{3,2,1,0:T(8,128)(2,1)S(1)}, bf16[1,2,1536,384]{3,2,1,0:T(8,128)(2,1)}, u32[]{:S(2)}) copy-start(bf16[1,2,1536,384]{3,2,1,0:T(8,128)(2,1)} %param.6) | copy-start | bytes 7077892
  45.9 13.5 %collective-permute-start.6 = (bf16[2,192,384]{2,1,0:T(8,128)(2,1)}, bf16[2,192,384]{2,1,0:T(8,128)(2,1)}, u32[]{:S(2)}, u32[]{:S(2)}) collective-permute-start(bf16[2,192,384]{2,1,0:T(8,128)(2,1)} %broadcast_select_fusion.1), channel_id=1, source_target_pairs={{0,1},{1,0},{2,3},{3,2},{4,5},{5,4},{6,7},{7,6},{8,9},{9,8},{10,11... | collective-permute-start | bytes 884744 | tf_op jit(solution)/shard_map/ppermute | solution.py:529
  51.6 10.1 %collective-permute-start.7 = (bf16[2,192,384]{2,1,0:T(8,128)(2,1)}, bf16[2,192,384]{2,1,0:T(8,128)(2,1)}, u32[]{:S(2)}, u32[]{:S(2)}) collective-permute-start(bf16[2,192,384]{2,1,0:T(8,128)(2,1)} %broadcast_select_fusion), channel_id=1, source_target_pairs={{0,1},{1,0},{2,3},{3,2},{4,5},{5,4},{6,7},{7,6},{8,9},{9,8},{10,11... | collective-permute-start | bytes 884744 | tf_op jit(solution)/shard_map/ppermute | solution.py:529
  53.4 68.9 %collective-permute-start.16 = (bf16[2,384,384]{2,1,0:T(8,128)(2,1)}, bf16[2,384,384]{2,1,0:T(8,128)(2,1)}, u32[]{:S(2)}, u32[]{:S(2)}) collective-permute-start(bf16[2,384,384]{2,1,0:T(8,128)(2,1)} %pick.1), channel_id=1, source_target_pairs={{0,12},{12,0},{1,13},{13,1},{2,14},{14,2},{3,15},{15,3},{16,28},{2... | collective-permute-start | bytes 1769480 | tf_op jit(solution)/shard_map/ppermute | solution.py:529
  57.2 65.1 %collective-permute-start.15 = (bf16[2,384,384]{2,1,0:T(8,128)(2,1)}, bf16[2,384,384]{2,1,0:T(8,128)(2,1)}, u32[]{:S(2)}, u32[]{:S(2)}) collective-permute-start(bf16[2,384,384]{2,1,0:T(8,128)(2,1)} %pick.1), channel_id=1, source_target_pairs={{4,8},{8,4},{5,9},{9,5},{6,10},{10,6},{7,11},{11,7},{20,24},{24,20... | collective-permute-start | bytes 1769480 | tf_op jit(solution)/shard_map/ppermute | solution.py:529
  58.7 28.7 %collective-permute-start.12 = (bf16[2,384,384]{2,1,0:T(8,128)(2,1)}, bf16[2,384,384]{2,1,0:T(8,128)(2,1)}, u32[]{:S(2)}, u32[]{:S(2)}) collective-permute-start(bf16[2,384,384]{2,1,0:T(8,128)(2,1)} %copy-done.6), channel_id=1, source_target_pairs={{0,4},{12,8},{4,0},{8,12},{1,5},{13,9},{5,1},{9,13},{2,6},{14,10},... | collective-permute-start | bytes 1769480 | tf_op jit(solution)/shard_map/ppermute | solution.py:529
  59.4 50.3 %collective-permute-start.14 = (bf16[2,384,384]{2,1,0:T(8,128)(2,1)}, bf16[2,384,384]{2,1,0:T(8,128)(2,1)S(1)}, u32[]{:S(2)}, u32[]{:S(2)}) collective-permute-start(bf16[2,384,384]{2,1,0:T(8,128)(2,1)} %copy-done.5), channel_id=1, source_target_pairs={{4,12},{8,0},{5,13},{9,1},{6,14},{10,2},{7,15},{11,3},{20,28},{24,... | collective-permute-start | bytes 1769480 | tf_op jit(solution)/shard_map/ppermute | solution.py:529
  61.7 53.4 %collective-permute-start.13 = (bf16[2,384,384]{2,1,0:T(8,128)(2,1)}, bf16[2,384,384]{2,1,0:T(8,128)(2,1)S(1)}, u32[]{:S(2)}, u32[]{:S(2)}) collective-permute-start(bf16[2,384,384]{2,1,0:T(8,128)(2,1)} %copy-done.5), channel_id=1, source_target_pairs={{0,8},{12,4},{1,9},{13,5},{2,10},{14,6},{3,11},{15,7},{16,24},{28,... | collective-permute-start | bytes 1769480 | tf_op jit(solution)/shard_map/ppermute | solution.py:529
  87.5 23.7 %collective-permute-start.8 = (bf16[2,96,384]{2,1,0:T(8,128)(2,1)S(1)}, bf16[2,96,384]{2,1,0:T(8,128)(2,1)S(1)}, u32[]{:S(2)}, u32[]{:S(2)}) collective-permute-start(bf16[2,96,384]{2,1,0:T(8,128)(2,1)S(1)} %constant_dynamic-slice_fusion.1), channel_id=1, source_target_pairs={{0,2},{2,0},{1,3},{3,1},{4,6},{6,4},{5,7},{7,5},{8,10},{10,8},{9,1... | collective-permute-start | bytes 442376 | tf_op jit(solution)/shard_map/ppermute | solution.py:529
  109.7 5.4 %collective-permute-start.9 = (bf16[2,96,384]{2,1,0:T(8,128)(2,1)S(1)}, bf16[2,96,384]{2,1,0:T(8,128)(2,1)S(1)}, u32[]{:S(2)}, u32[]{:S(2)}) collective-permute-start(bf16[2,96,384]{2,1,0:T(8,128)(2,1)S(1)} %constant_dynamic-slice_fusion), channel_id=1, source_target_pairs={{0,2},{2,0},{1,3},{3,1},{4,6},{6,4},{5,7},{7,5},{8,10},{10,8},{9,1... | collective-permute-start | bytes 442376 | tf_op jit(solution)/shard_map/ppermute | solution.py:529
  111.2 3.9 %collective-permute-start.10 = (bf16[2,96,384]{2,1,0:T(8,128)(2,1)S(1)}, bf16[2,96,384]{2,1,0:T(8,128)(2,1)S(1)}, u32[]{:S(2)}, u32[]{:S(2)}) collective-permute-start(bf16[2,96,384]{2,1,0:T(8,128)(2,1)S(1)} %collective-permute-done.8.refs_6_), channel_id=1, source_target_pairs={{0,1},{1,0},{2,3},{3,2},{4,5},{5,4},{6,7},{7,6},{8,9},{9,8},{10,11... | collective-permute-start | bytes 442376 | tf_op jit(solution)/shard_map/ppermute | solution.py:529
  115.1 1.4 %collective-permute-start.11 = (bf16[2,96,384]{2,1,0:T(8,128)(2,1)S(1)}, bf16[2,96,384]{2,1,0:T(8,128)(2,1)S(1)}, u32[]{:S(2)}, u32[]{:S(2)}) collective-permute-start(bf16[2,96,384]{2,1,0:T(8,128)(2,1)S(1)} %collective-permute-done.9.refs_7_), channel_id=1, source_target_pairs={{0,1},{1,0},{2,3},{3,2},{4,5},{5,4},{6,7},{7,6},{8,9},{9,8},{10,11... | collective-permute-start | bytes 442376 | tf_op jit(solution)/shard_map/ppermute | solution.py:529
